TPU v7x, 32 devices: a whole 2x2x4 slice. The times are simulated.
32 devices in a mesh: tile: 16 (over z, x, core), mem: 2 (over y).
Axes of the slice: x: 2, y: 2, z: 4, core: 2. Of those that a mesh axis runs over, the one named last changes fastest.
Arguments:
- ensemble: float32 [64, 7, 32768], P('mem', None, 'tile'), may hold values from -6 to 6
- obs_site: int32 [8, 32], replicated, may hold values from 0 to 14335
- obs_value: float32 [8, 32], replicated, may hold values from -8 to 8
- obs_var: float32 [8, 32], replicated, may hold values from 4 to 32
- owner_tile: int32 [8], replicated, may hold values from 0 to 15
- tile_mask: int32 [8, 16], replicated, may hold values 0 or 1
- batch_order: int32 [8], replicated, may hold values from 0 to 7, each once
Outputs:
- posterior: float32 [64, 7, 32768], P('mem', None, 'tile')
All inputs are finite; a program needn't handle non-finite values.
Results may differ from a plain program's by a relative error of at most 0.0001.
Values sent between devices are 32-bit elements; how exact they have to be, the bound alone decides.
No kernel may reach another device: no remote copies, remote signals or barrier semaphores. Data moves between devices by JAX's collectives and lax.ppermute only.
A program may use at most 64 MiB of HBM per device.

v0:
```python
import functools

import jax
import jax.numpy as jnp
from jax import lax
from jax.experimental import pallas as pl
from jax.experimental.pallas import tpu as pltpu
from jax.sharding import PartitionSpec as P


LANES = 128
SUBS = 8
SMEM = pl.BlockSpec(memory_space=pltpu.SMEM)
VMEM = pl.BlockSpec(memory_space=pltpu.VMEM)
ANY = pl.BlockSpec(memory_space=pl.ANY)


def hbm(x):
    return pltpu.with_memory_space_constraint(x, pltpu.HBM)


def vmem(x):
    return pltpu.with_memory_space_constraint(x, pltpu.VMEM)


def first_kernel(units_hbm, first_ref, sem):
    copy = pltpu.make_async_copy(units_hbm.at[pl.ds(0, first_ref.shape[0])], first_ref, sem)
    copy.start()
    copy.wait()


def first_units(units, count):
    return pl.pallas_call(
        first_kernel,
        out_shape=pltpu.VMEM((count,) + units.shape[1:], jnp.float32),
        in_specs=[ANY],
        out_specs=VMEM,
        scratch_shapes=[pltpu.SemaphoreType.DMA],
        name="first_units",
    )(hbm(units))


def split(value, size):
    if size & (size - 1) == 0:
        return lax.shift_right_logical(value, size.bit_length() - 1), lax.bitwise_and(value, size - 1)
    quotient = lax.div(value, size)
    return quotient, value - quotient * size


def gather_kernel(site_hbm, owner_hbm, order_hbm, units_hbm, first_ref, rows_ref, main_ref, last_ref,
                  site_ref, owner_ref, order_ref, sem):
    batches, obs = site_hbm.shape
    count, half, cells = units_hbm.shape
    per = LANES // obs
    head, middle, tail = first_ref.shape[0], main_ref.shape[0], last_ref.shape[0]
    copies = [
        pltpu.make_async_copy(owner_hbm, owner_ref, sem.at[0]),
        pltpu.make_async_copy(order_hbm, order_ref, sem.at[1]),
        pltpu.make_async_copy(site_hbm, site_ref, sem.at[2]),
        pltpu.make_async_copy(units_hbm.at[pl.ds(head, middle)], main_ref, sem.at[3]),
        pltpu.make_async_copy(units_hbm.at[pl.ds(count - tail, tail)], last_ref, sem.at[4]),
    ]
    for copy in copies:
        copy.start()
    tile = lax.axis_index("tile")
    lane = lax.broadcasted_iota(jnp.int32, (half, LANES), 1)
    rows_ref[...] = jnp.zeros_like(rows_ref)
    for copy in copies:
        copy.wait()

    def one(p, carry):
        b = order_ref[p]

        @pl.when(owner_ref[b] == tile)
        def _():
            group, place = split(p, per)
            base = place * obs
            spot = pl.ds(pl.multiple_of(group * LANES, LANES), LANES)
            acc = [rows_ref[h * half:(h + 1) * half, spot] for h in range(2)]
            for k in range(obs):
                chan, cell = split(site_ref[b, k], cells)
                _, col = split(cell, LANES)
                here = pl.ds(pl.multiple_of(cell - col, LANES), LANES)
                at = base + k
                turn = lax.bitwise_and(at - col, LANES - 1)
                mine = lane == at
                for h in range(2):
                    unit = 2 * chan + h
                    block = main_ref[jnp.clip(unit - head, 0, middle - 1), :, here]
                    early = first_ref[jnp.minimum(unit, head - 1), :, here]
                    late = last_ref[jnp.clip(unit - (count - tail), 0, tail - 1), :, here]
                    block = jnp.where(unit < head, early, jnp.where(unit >= count - tail, late, block))
                    acc[h] = jnp.where(mine, pltpu.roll(block, turn, 1), acc[h])
            for h in range(2):
                rows_ref[h * half:(h + 1) * half, spot] = acc[h]

        return carry

    lax.fori_loop(0, batches, one, 0)


def gather_rows(units, first, obs_site, owner_tile, batch_order, tail):
    batches, obs = obs_site.shape
    count, half, cells = units.shape
    f32 = jnp.float32
    return pl.pallas_call(
        gather_kernel,
        out_shape=(
            pltpu.VMEM((2 * half, batches * obs), f32),
            pltpu.VMEM((count - first.shape[0] - tail, half, cells), f32),
            pltpu.VMEM((tail, half, cells), f32),
        ),
        in_specs=[ANY] * 4 + [VMEM],
        out_specs=(VMEM, VMEM, VMEM),
        scratch_shapes=[
            pltpu.SMEM(obs_site.shape, jnp.int32),
            pltpu.SMEM(owner_tile.shape, jnp.int32),
            pltpu.SMEM(batch_order.shape, jnp.int32),
            pltpu.SemaphoreType.DMA((5,)),
        ],
        compiler_params=pltpu.CompilerParams(vmem_limit_bytes=8 << 20),
        name="gather_rows",
    )(hbm(obs_site), hbm(owner_tile), hbm(batch_order), hbm(units), vmem(first))


def spread(row):
    return jnp.broadcast_to(row, (SUBS, row.shape[1]))


def thirds(x):
    parts = []
    for _ in range(3):
        parts.append(x.astype(jnp.bfloat16))
        x = x - parts[-1].astype(jnp.float32)
    return parts


def left_factor(mat):
    high, mid, low = thirds(mat)
    zero = jnp.zeros_like(low)
    return jnp.concatenate([
        jnp.concatenate([high, high, high], axis=1),
        jnp.concatenate([mid, mid, zero], axis=1),
        jnp.concatenate([low, zero, zero], axis=1),
    ], axis=0)


def chain_kernel(order_ref, owner_ref, mask_ref, var_ref, tile_ref, part_ref, back_ref, val_ref,
                 out_ref, mine_ref, theirs_ref, w_ref, left_ref, right_ref, z_ref, v_ref, val_s, cov_ref):
    batches, obs = val_ref.shape
    members = part_ref.shape[0]
    half = members // 2
    total = batches * obs
    tiles = total // LANES
    per = LANES // obs
    blocks = obs // SUBS
    width = w_ref.shape[0]
    inv = 1.0 / (members - 1)
    highest = lax.Precision.HIGHEST
    contract = functools.partial(
        lax.dot_general, dimension_numbers=(((0,), (0,)), ((), ())), precision=highest,
        preferred_element_type=jnp.float32)
    lane1 = lax.broadcasted_iota(jnp.int32, (1, LANES), 1)
    lane8 = lax.broadcasted_iota(jnp.int32, (SUBS, LANES), 1)
    sub8 = lax.broadcasted_iota(jnp.int32, (SUBS, LANES), 0)
    tile = tile_ref[0]

    val_s[...] = jnp.zeros_like(val_s)
    val_s[:, :obs] = val_ref[...]
    values = []
    for t in range(tiles):
        row = jnp.zeros((1, LANES), jnp.float32)
        for q in range(per):
            one = val_s[pl.ds(order_ref[t * per + q], 1), :]
            row = row + (pltpu.roll(one, q * obs, 1) if q else one)
        values.append(row)
    values = jnp.concatenate(values, axis=1)

    part, back = part_ref[...], back_ref[...]
    even = lax.rem(tile, 2) == 0
    raw = jnp.concatenate([jnp.where(even, part, back), jnp.where(even, back, part)], axis=1)
    mean = jnp.sum(raw, axis=0, keepdims=True) * (1.0 / members)
    anom = raw - mean
    first = lax.broadcasted_iota(jnp.int32, (SUBS, total), 0) == 0
    lhs = jnp.concatenate([anom, jnp.where(first, values - mean, 0.0)], axis=0)
    depth = members + SUBS
    r_i = lax.broadcasted_iota(jnp.int32, (depth, 2 * LANES), 0)
    l_i = lax.broadcasted_iota(jnp.int32, (depth, 2 * LANES), 1)
    pick = jnp.where((r_i < members) & ((l_i == r_i) | (l_i == r_i + members)), 1.0, 0.0)
    pick = jnp.where((r_i == members) & (l_i == LANES), 1.0, pick)
    rhs = jnp.concatenate(
        [jnp.concatenate([anom, jnp.zeros((SUBS, total), jnp.float32)], axis=0), pick], axis=1)
    full = contract(lhs, rhs)
    for t in range(width):
        w_ref[t] = full[:, t * LANES:(t + 1) * LANES]

    def batch(p, carry):
        b = order_ref[p]
        o = owner_ref[b]
        mine = (mask_ref[b, tile] == 1) | (o == tile)
        mine_f = jnp.where(mine, 1.0, 0.0)
        act = []
        late = []
        for t in range(tiles):
            row = jnp.zeros((1, LANES), jnp.float32)
            row_late = jnp.zeros((1, LANES), jnp.float32)
            for q in range(per):
                other = owner_ref[order_ref[t * per + q]]
                on = (mask_ref[b, other] == 1) | (o == other)
                here = (lane1 >= q * obs) & (lane1 < (q + 1) * obs)
                row = jnp.where(here, jnp.where(on, 1.0, 0.0), row)
                row_late = jnp.where(here, jnp.where(t * per + q > p, 1.0, 0.0), row_late)
            act.append(row)
            late.append(row_late)
        act8 = [spread(a) > 0.5 for a in act]
        z_on = jnp.where(lane8 < members, mine_f, 0.0) > 0.5
        pick_w = act8 + [z_on, lane8 == 0]
        pick_b = act8 + [z_on, lane8 < 0]

        start = pl.multiple_of(p * obs, obs)
        rows = pl.ds(start, obs)
        wp = [[w_ref[t, pl.ds(pl.multiple_of(start + i * SUBS, SUBS), SUBS), :] for i in range(blocks)]
              for t in range(width)]
        shift = lax.rem(LANES - lax.rem(p, per) * obs, LANES)
        gram = w_ref[lax.div(p, per), rows, :] * inv
        gram = pltpu.roll(gram, shift, 1)
        cols = [[jnp.broadcast_to(gram[i * SUBS:(i + 1) * SUBS, j:j + 1], (SUBS, LANES)) if i >= j // SUBS else None
                 for i in range(blocks)] for j in range(obs)]
        gains, alphas = [], []
        for e in range(blocks):
            gain8 = jnp.zeros((SUBS, LANES), jnp.float32)
            ratio8 = jnp.zeros((SUBS, LANES), jnp.float32)
            scaled = []
            for r in range(SUBS):
                k = e * SUBS + r
                col = cols[k]
                var = var_ref[b, k]
                g = 1.0 / (spread(col[e][r:r + 1, :]) + var)
                gain8 = jnp.where(sub8 == r, g, gain8)
                ratio8 = jnp.where(sub8 == r, var * g, ratio8)
                scale = [None] * e + [col[i] * g for i in range(e, blocks)]
                for i in range(e, blocks):
                    cov_ref[k, i * SUBS:(i + 1) * SUBS, :] = col[i]
                for n in range(k + 1, obs):
                    if n == k + 1:
                        factor = spread(col[n // SUBS][n % SUBS:n % SUBS + 1, :])
                    else:
                        factor = cov_ref[k, pl.ds(n, SUBS, stride=0), :]
                    for i in range(n // SUBS, blocks):
                        cols[n][i] = cols[n][i] - scale[i] * factor
                scale[e] = jnp.where(sub8 > r, scale[e], 0.0)
                scaled.append(scale)
            alpha8 = 1.0 / (1.0 + jnp.sqrt(ratio8))
            gains.append(gain8)
            alphas.append(alpha8)
            for r in range(SUBS):
                alpha = spread(alpha8[r:r + 1, :])
                for t in range(width):
                    u = spread(wp[t][e][r:r + 1, :])
                    both = jnp.where(pick_w[t], u, alpha * u)
                    for i in range(e, blocks):
                        wp[t][i] = wp[t][i] - scaled[r][i] * both
        for i in range(blocks):
            gain = gains[i] * inv
            alpha = alphas[i]
            own = slice(i * SUBS, (i + 1) * SUBS)
            off = slice(obs + i * SUBS, obs + (i + 1) * SUBS)
            for t in range(width):
                here = slice(t * LANES, (t + 1) * LANES)
                reduced = alpha * wp[t][i]
                right_ref[own, here] = jnp.where(pick_w[t], wp[t][i], reduced)
                right_ref[off, here] = jnp.where(pick_b[t], reduced, 0.0)
                if t < tiles:
                    d = wp[t][i] * (late[t] * gain)
                    left_ref[own, here] = d * act[t]
                    left_ref[off, here] = d * (1.0 - act[t])
            at = pl.ds(pl.multiple_of(start + i * SUBS, SUBS), SUBS)
            z_ref[at, :] = wp[tiles][i] * mine_f
            miss = jnp.broadcast_to(wp[width - 1][i][:, :1], (SUBS, LANES))
            v_ref[at, :] = (miss - alpha * wp[tiles][i]) * gain

        for low in range(tiles):
            @pl.when((p < batches - 1) & (lax.div(p + 1, per) == low))
            def _():
                update = contract(left_ref[:, low * LANES:], right_ref[:, low * LANES:])
                for t in range(low, width):
                    w_ref[t, low * LANES:, :] = w_ref[t, low * LANES:, :] - update[:, (t - low) * LANES:(t - low + 1) * LANES]

        return carry

    lax.fori_loop(0, batches, batch, 0)
    moved = contract(v_ref[...], z_ref[...])
    mat = moved[members:members + half, :members]
    out_ref[...] = left_factor(mat)
    mine_ref[...] = left_factor(mat[:, :half])
    theirs_ref[...] = left_factor(mat[:, half:])


def chain(part, back, obs_value, obs_var, owner_tile, tile_mask, batch_order, tile):
    members, total = part.shape[0], 2 * part.shape[1]
    half = members // 2
    obs = obs_value.shape[1]
    width = total // LANES + 2
    f32 = jnp.float32
    return pl.pallas_call(
        chain_kernel,
        out_shape=[pltpu.VMEM((3 * half, 3 * k), jnp.bfloat16) for k in (members, half, half)],
        in_specs=[SMEM] * 5 + [VMEM] * 3,
        out_specs=[VMEM] * 3,
        scratch_shapes=[
            pltpu.VMEM((width, total, LANES), f32),
            pltpu.VMEM((2 * obs, total), f32),
            pltpu.VMEM((2 * obs, width * LANES), f32),
            pltpu.VMEM((total, LANES), f32),
            pltpu.VMEM((total, LANES), f32),
            pltpu.VMEM((obs_value.shape[0], LANES), f32),
            pltpu.VMEM((obs, obs, LANES), f32),
        ],
        compiler_params=pltpu.CompilerParams(vmem_limit_bytes=8 << 20),
        name="chain",
    )(batch_order, owner_tile, tile_mask, obs_var, tile, vmem(part), vmem(back), obs_value)


def times(left, x):
    half = left.shape[0] // 3
    y = jnp.dot(left, jnp.concatenate(thirds(x), axis=0), preferred_element_type=jnp.float32)
    return (y[2 * half:] + y[half:2 * half]) + y[:half]


def apply_block(left, own, upper, lower):
    return own + times(left, jnp.concatenate([own, upper, lower], axis=0))


def apply_main(mat_ref, mine_ref, own_first_ref, own_main_ref, own_last_ref, first_ref, main_ref, out_hbm, part_ref,
               new_ref, sem_out):
    chans = new_ref.shape[0]
    ahead = first_ref.shape[0]
    stores = [pltpu.make_async_copy(new_ref.at[c], out_hbm.at[c], sem_out.at[c]) for c in range(chans)]
    left = mat_ref[...]

    def pair(a, b, c):
        return [a[u] if u < ahead else b[u - ahead] for u in (2 * c, 2 * c + 1)]

    for c in range(chans):
        own = jnp.concatenate(pair(own_first_ref, own_main_ref, c), axis=0)
        new_ref[c] = apply_block(left, own, *pair(first_ref, main_ref, c))
        stores[c].start()
    for c in range(part_ref.shape[0]):
        own = jnp.concatenate([own_last_ref[2 * c], own_last_ref[2 * c + 1]], axis=0)
        part_ref[c] = own + times(mine_ref[...], own)
    for store in stores:
        store.wait()


def apply_last(theirs_ref, part_ref, last_ref, prev_hbm, out_hbm, new_ref, sem_out):
    chans, _, cells = new_ref.shape
    start = out_hbm.shape[0] - chans
    cuts = sem_out.shape[1]
    wide = cells // cuts
    left = theirs_ref[...]
    stores = []
    for c in range(chans):
        for q in range(cuts):
            here = pl.ds(q * wide, wide)
            oth = jnp.concatenate([last_ref[2 * c, :, here], last_ref[2 * c + 1, :, here]], axis=0)
            new_ref[c, :, here] = part_ref[c, :, here] + times(left, oth)
            stores.append(
                pltpu.make_async_copy(new_ref.at[c, :, here], out_hbm.at[start + c, :, here], sem_out.at[c, q]))
            stores[-1].start()
    for store in stores:
        store.wait()


def apply_matrix(mat, mine, theirs, shape, own_first, own_main, own_last, first, main, last):
    chans, half, cells = shape
    tail = last.shape[0] // 2
    head = chans - tail
    f32 = jnp.float32
    state = pltpu.HBM(shape, f32)
    params = pltpu.CompilerParams(vmem_limit_bytes=8 << 20)
    out, part = pl.pallas_call(
        apply_main,
        out_shape=(state, pltpu.VMEM((tail, half, cells), f32)),
        in_specs=[VMEM] * 7,
        out_specs=(ANY, VMEM),
        scratch_shapes=[pltpu.VMEM((head, half, cells), f32), pltpu.SemaphoreType.DMA((head,))],
        compiler_params=params,
        name="apply_main",
    )(vmem(mat), vmem(mine), vmem(own_first), vmem(own_main), vmem(own_last), vmem(first), vmem(main))
    return pl.pallas_call(
        apply_last,
        out_shape=state,
        in_specs=[VMEM, VMEM, VMEM, ANY],
        out_specs=ANY,
        input_output_aliases={3: 0},
        scratch_shapes=[pltpu.VMEM((tail, half, cells), f32), pltpu.SemaphoreType.DMA((tail, 4))],
        compiler_params=params,
        name="apply_last",
    )(vmem(theirs), vmem(part), vmem(last), hbm(out))


def body(ensemble, obs_site, obs_value, obs_var, owner_tile, tile_mask, batch_order):
    tile = lax.axis_index("tile").astype(jnp.int32).reshape(1)
    n_tile = lax.axis_size("tile")
    swap = [(0, 1), (1, 0)]
    ens = jnp.transpose(ensemble, (1, 0, 2))
    chans, half, cells = ens.shape
    units = ens.reshape(2 * chans, half // 2, cells)
    head, tail = 4, 2

    def across(x, step):
        return lax.ppermute(x, "tile", [(i, i ^ step) for i in range(n_tile)])

    own_first = first_units(units, head)
    first = lax.ppermute(own_first, "mem", swap)
    own, own_main, own_last = gather_rows(units, own_first, obs_site, owner_tile, batch_order, tail)
    own = own + across(own, 1)
    cut = own.shape[1] // 2
    own = jnp.where(lax.rem(tile[0], 2) == 0, own[:, :cut], own[:, cut:])
    own = own + across(own, 2)
    low = lax.rem(lax.div(tile[0], 2), 2) == 0
    cut = own.shape[0] // 2
    own = jnp.where(low, own[:cut], own[cut:])
    oth = lax.ppermute(own, "mem", swap)
    main = lax.ppermute(own_main, "mem", swap)
    last = lax.ppermute(own_last, "mem", swap)
    part = jnp.concatenate([own, oth], axis=0)
    step = 4
    while step < n_tile:
        part = part + across(part, step)
        step *= 2
    other = lax.ppermute(part, "tile", [(i, i ^ 2) for i in range(n_tile)])
    upper, lower = jnp.where(low, part, other), jnp.where(low, other, part)
    part = jnp.concatenate([upper[:cut], lower[:cut], upper[cut:], lower[cut:]], axis=0)
    back = lax.ppermute(part, "tile", [(i, i ^ 1) for i in range(n_tile)])
    mat, mine, theirs = chain(part, back, obs_value, obs_var, owner_tile, tile_mask, batch_order, tile)
    out = apply_matrix(mat, mine, theirs, ens.shape, own_first, own_main, own_last, first, main, last)
    return jnp.transpose(out, (1, 0, 2))


def solution(mesh):
    return jax.shard_map(
        body,
        mesh=mesh,
        in_specs=(P("mem", None, "tile"), P(), P(), P(), P(), P(), P()),
        out_specs=P("mem", None, "tile"),
        check_vma=False,
    )
```

profile of v0, /device:TPU:0, one launch (start us, length us, event | category | flops | bytes accessed | tf_op | source)
XLA Modules:
  0.0 59.5 jit_solution(9708274021442557950)
XLA Ops:
  0.0 1.0 %first_units.1.first_ref.own_first_ref = f32[4,16,2048]{2,1,0:T(8,128)S(1)} custom-call(f32[14,16,2048]{2,1,0:T(8,128)} %bitcast.5), custom_call_target="tpu_custom_call" | custom-call | tf_op jit(solution)/shard_map/first_units/pallas_call | solution.py:33
  1.1 0.0 copy-start
  1.1 0.0 copy-start.1
  1.1 0.0 copy-start.2
  1.1 0.0 copy-start.3
  1.1 0.0 copy-start.4
  1.1 2.0 %gather_rows.1 = (f32[32,256]{1,0:T(8,128)S(1)}, f32[8,16,2048]{2,1,0:T(8,128)S(1)}, f32[2,16,2048]{2,1,0:T(8,128)S(1)}) custom-call(s32[8,32]{1,0:T(8,128)} %site_hbm.1, s32[8]{0:T(128)} %owner_ref.1, s32[8]{0:T(128)} %order_ref.1, f32[14,16,2048]{2,1,0:T(8,128)} %bitcast.6, f32[4,16,2048]{2,1,0:T(8,128)S(1)} %first_units.1.first_ref.own_first_ref), custom_call_target="tpu_custom_call" | custom-call | tf_op jit(solution)/shard_map/gather_rows/pallas_call | solution.py:106
  3.1 0.6 collective-permute-start
  3.7 0.9 %collective-permute-done = f32[32,256]{1,0:T(8,128)S(1)} collective-permute-done((f32[32,256]{1,0:T(8,128)S(1)}, f32[32,256]{1,0:T(8,128)S(1)}, u32[]{:S(2)}, u32[]{:S(2)}) %collective-permute-start) | collective-permute-done | bytes 32800 | tf_op jit(solution)/shard_map/ppermute | solution.py:412
  4.6 2.2 %collective-permute-start.1 = (f32[32,128]{1,0:T(8,128)S(1)}, f32[32,128]{1,0:T(8,128)S(1)}, u32[]{:S(2)}, u32[]{:S(2)}) collective-permute-start(f32[32,128]{1,0:T(8,128)S(1)} %slice_select_fusion), channel_id=1, source_target_pairs={{0,4},{2,6},{4,0},{6,2},{8,12},{10,14},{12,8},{14,10},{16,20},{18,... | collective-permute-start | bytes 49160 | tf_op jit(solution)/shard_map/ppermute | solution.py:412
  6.8 1.5 %collective-permute-start.8 = (f32[8,16,2048]{2,1,0:T(8,128)S(1)}, f32[8,16,2048]{2,1,0:T(8,128)S(1)}, u32[]{:S(2)}, u32[]{:S(2)}) collective-permute-start(f32[8,16,2048]{2,1,0:T(8,128)S(1)} %get-tuple-element.17.own_main_ref), channel_id=1, source_target_pairs={{0,1},{1,0},{2,3},{3,2},{4,5},{5,4},{6,7},{7,6},{8,9},{9,8},{10,11... | collective-permute-start | bytes 3145736 | tf_op jit(solution)/shard_map/ppermute | solution.py:425
  8.3 0.2 collective-permute-done.1
  8.5 2.8 %collective-permute-start.2 = (f32[16,128]{1,0:T(8,128)S(1)}, f32[16,128]{1,0:T(8,128)S(1)}, u32[]{:S(2)}, u32[]{:S(2)}) collective-permute-start(f32[16,128]{1,0:T(8,128)S(1)} %slice_select_fusion.1), channel_id=1, source_target_pairs={{0,1},{1,0},{2,3},{3,2},{4,5},{5,4},{6,7},{7,6},{8,9},{9,8},{10,11... | collective-permute-start | bytes 24584 | tf_op jit(solution)/shard_map/ppermute | solution.py:424
  11.3 20.6 %collective-permute-done.2 = f32[16,128]{1,0:T(8,128)S(1)} collective-permute-done((f32[16,128]{1,0:T(8,128)S(1)}, f32[16,128]{1,0:T(8,128)S(1)}, u32[]{:S(2)}, u32[]{:S(2)}) %collective-permute-start.2) | collective-permute-done | bytes 8224 | tf_op jit(solution)/shard_map/ppermute | solution.py:424
  31.9 2.0 %collective-permute-start.3 = (f32[32,128]{1,0:T(8,128)S(1)}, f32[32,128]{1,0:T(8,128)S(1)}, u32[]{:S(2)}, u32[]{:S(2)}) collective-permute-start(f32[32,128]{1,0:T(8,128)S(1)} %pad_maximum_fusion.1), channel_id=1, source_target_pairs={{0,8},{2,10},{4,12},{6,14},{8,0},{10,2},{12,4},{14,6},{16,24},{18,... | collective-permute-start | bytes 49160 | tf_op jit(solution)/shard_map/ppermute | solution.py:412
  33.9 1.8 %collective-permute-done.3 = f32[32,128]{1,0:T(8,128)S(1)} collective-permute-done((f32[32,128]{1,0:T(8,128)S(1)}, f32[32,128]{1,0:T(8,128)S(1)}, u32[]{:S(2)}, u32[]{:S(2)}) %collective-permute-start.3) | collective-permute-done | bytes 16416 | tf_op jit(solution)/shard_map/ppermute | solution.py:412
  35.6 3.0 %collective-permute-start.4 = (f32[32,128]{1,0:T(8,128)S(1)}, f32[32,128]{1,0:T(8,128)S(1)}, u32[]{:S(2)}, u32[]{:S(2)}) collective-permute-start(f32[32,128]{1,0:T(8,128)S(1)} %fusion), channel_id=1, source_target_pairs={{0,16},{2,18},{4,20},{6,22},{8,24},{10,26},{12,28},{14,30},{16,0},... | collective-permute-start | bytes 49160 | tf_op jit(solution)/shard_map/ppermute | solution.py:412
  38.6 1.7 %collective-permute-done.4 = f32[32,128]{1,0:T(8,128)S(1)} collective-permute-done((f32[32,128]{1,0:T(8,128)S(1)}, f32[32,128]{1,0:T(8,128)S(1)}, u32[]{:S(2)}, u32[]{:S(2)}) %collective-permute-start.4) | collective-permute-done | bytes 16416 | tf_op jit(solution)/shard_map/ppermute | solution.py:412
  40.3 1.0 %collective-permute-start.5 = (f32[32,128]{1,0:T(8,128)S(1)}, f32[32,128]{1,0:T(8,128)S(1)}, u32[]{:S(2)}, u32[]{:S(2)}) collective-permute-start(f32[32,128]{1,0:T(8,128)S(1)} %add.15), channel_id=1, source_target_pairs={{0,4},{2,6},{4,0},{6,2},{8,12},{10,14},{12,8},{14,10},{16,20},{18,... | collective-permute-start | bytes 49160 | tf_op jit(solution)/shard_map/ppermute | solution.py:432
  41.3 1.7 %collective-permute-start.7 = (f32[4,16,2048]{2,1,0:T(8,128)S(1)}, f32[4,16,2048]{2,1,0:T(8,128)S(1)}, u32[]{:S(2)}, u32[]{:S(2)}) collective-permute-start(f32[4,16,2048]{2,1,0:T(8,128)S(1)} %first_units.1.first_ref.own_first_ref), channel_id=1, source_target_pairs={{0,1},{1,0},{2,3},{3,2},{4,5},{5,4},{6,7},{7,6},{8,9},{9,8},{10,11... | collective-permute-start | bytes 1572872 | tf_op jit(solution)/shard_map/ppermute | solution.py:415
  43.0 0.3 collective-permute-start.9
  43.3 0.7 %collective-permute-done.5 = f32[32,128]{1,0:T(8,128)S(1)} collective-permute-done((f32[32,128]{1,0:T(8,128)S(1)}, f32[32,128]{1,0:T(8,128)S(1)}, u32[]{:S(2)}, u32[]{:S(2)}) %collective-permute-start.5) | collective-permute-done | bytes 16416 | tf_op jit(solution)/shard_map/ppermute | solution.py:432
  44.1 0.1 collective-permute-start.6
  44.2 1.2 %collective-permute-done.6.back_ref = f32[64,128]{1,0:T(8,128)S(1)} collective-permute-done((f32[64,128]{1,0:T(8,128)S(1)}, f32[64,128]{1,0:T(8,128)S(1)}, u32[]{:S(2)}, u32[]{:S(2)}) %collective-permute-start.6) | collective-permute-done | bytes 32800 | tf_op jit(solution)/shard_map/ppermute | solution.py:435
  45.4 0.0 copy-done
  45.4 0.0 copy-done.1
  45.4 0.0 copy-done.2
  45.4 0.0 copy-done.3
  45.4 0.0 copy-done.4
  45.4 11.4 %chain.1 = (bf16[96,192]{1,0:T(8,128)(2,1)S(1)}, bf16[96,96]{1,0:T(8,128)(2,1)S(1)}, bf16[96,96]{1,0:T(8,128)(2,1)S(1)}) custom-call(s32[8]{0:T(128)S(1)} %copy-done.3, s32[8]{0:T(128)S(1)} %copy-done.4, s32[8,16]{1,0:T(8,128)S(1)} %copy-done, f32[8,32]{1,0:T(8,128)S(1)} %copy-done.1, s32[1]{0:T(128)} %bitcast.tile_ref, ...), custom_call_target="tpu_custom_call" | custom-call | tf_op jit(solution)/shard_map/chain/pallas_call | solution.py:305
  56.8 0.0 collective-permute-done.7.first_ref
  56.8 0.0 collective-permute-done.8.main_ref
  56.9 1.7 %apply_main.1 = (f32[7,32,2048]{2,1,0:T(8,128)}, f32[1,32,2048]{2,1,0:T(8,128)S(1)}) custom-call(bf16[96,192]{1,0:T(8,128)(2,1)S(1)} %get-tuple-element.15.mat_ref, bf16[96,96]{1,0:T(8,128)(2,1)S(1)} %get-tuple-element.16.mine_ref, f32[4,16,2048]{2,1,0:T(8,128)S(1)} %first_units.1.first_ref.own_first_ref, f32[8,16,2048]{2,1,0:T(8,128)S(1)} %get-tuple-element.17.own_main_ref, ...), custom_call_target="tpu_custom_call" | custom-call | tf_op jit(solution)/shard_map/apply_main/pallas_call | solution.py:381
  58.5 0.0 collective-permute-done.9.last_ref
  58.5 0.9 %apply_last.1 = f32[7,32,2048]{2,1,0:T(8,128)} custom-call(bf16[96,96]{1,0:T(8,128)(2,1)S(1)} %get-tuple-element.14.theirs_ref, f32[1,32,2048]{2,1,0:T(8,128)S(1)} %get-tuple-element.19.part_ref, f32[2,16,2048]{2,1,0:T(8,128)S(1)} %collective-permute-done.9.last_ref, f32[7,32,2048]{2,1,0:T(8,128)} %get-tuple-element.20.prev_hbm), custom_call_target="tpu_custom_call", output_to_operand_aliasing={{}: (3, {})} | custom-call | tf_op jit(solution)/shard_map/apply_last/pallas_call | solution.py:390
  (10 shorter events, 0.1 us)
Async XLA Ops:
  1.1 44.3 %copy-start = (s32[8,16]{1,0:T(8,128)S(1)}, s32[8,16]{1,0:T(8,128)}, u32[]{:S(2)}) copy-start(s32[8,16]{1,0:T(8,128)} %mask_ref.1) | copy-start | bytes 1540
  1.1 44.3 %copy-start.1 = (f32[8,32]{1,0:T(8,128)S(1)}, f32[8,32]{1,0:T(8,128)}, u32[]{:S(2)}) copy-start(f32[8,32]{1,0:T(8,128)} %var_ref.1) | copy-start | bytes 3076
  1.1 44.3 %copy-start.2 = (f32[8,32]{1,0:T(8,128)S(1)}, f32[8,32]{1,0:T(8,128)}, u32[]{:S(2)}) copy-start(f32[8,32]{1,0:T(8,128)} %val_ref.1) | copy-start | bytes 3076
  1.1 44.3 %copy-start.3 = (s32[8]{0:T(128)S(1)}, s32[8]{0:T(128)}, u32[]{:S(2)}) copy-start(s32[8]{0:T(128)} %order_ref.1) | copy-start | bytes 100
  1.1 44.3 %copy-start.4 = (s32[8]{0:T(128)S(1)}, s32[8]{0:T(128)}, u32[]{:S(2)}) copy-start(s32[8]{0:T(128)} %owner_ref.1) | copy-start | bytes 100
  3.1 1.4 %collective-permute-start = (f32[32,256]{1,0:T(8,128)S(1)}, f32[32,256]{1,0:T(8,128)S(1)}, u32[]{:S(2)}, u32[]{:S(2)}) collective-permute-start(f32[32,256]{1,0:T(8,128)S(1)} %get-tuple-element.13), channel_id=1, source_target_pairs={{0,2},{2,0},{4,6},{6,4},{8,10},{10,8},{12,14},{14,12},{16,18},{18,... | collective-permute-start | bytes 98312 | tf_op jit(solution)/shard_map/ppermute | solution.py:412
  4.6 3.9 %collective-permute-start.1 = (f32[32,128]{1,0:T(8,128)S(1)}, f32[32,128]{1,0:T(8,128)S(1)}, u32[]{:S(2)}, u32[]{:S(2)}) collective-permute-start(f32[32,128]{1,0:T(8,128)S(1)} %slice_select_fusion), channel_id=1, source_target_pairs={{0,4},{2,6},{4,0},{6,2},{8,12},{10,14},{12,8},{14,10},{16,20},{18,... | collective-permute-start | bytes 49160 | tf_op jit(solution)/shard_map/ppermute | solution.py:412
  6.8 50.1 %collective-permute-start.8 = (f32[8,16,2048]{2,1,0:T(8,128)S(1)}, f32[8,16,2048]{2,1,0:T(8,128)S(1)}, u32[]{:S(2)}, u32[]{:S(2)}) collective-permute-start(f32[8,16,2048]{2,1,0:T(8,128)S(1)} %get-tuple-element.17.own_main_ref), channel_id=1, source_target_pairs={{0,1},{1,0},{2,3},{3,2},{4,5},{5,4},{6,7},{7,6},{8,9},{9,8},{10,11... | collective-permute-start | bytes 3145736 | tf_op jit(solution)/shard_map/ppermute | solution.py:425
  8.5 23.4 %collective-permute-start.2 = (f32[16,128]{1,0:T(8,128)S(1)}, f32[16,128]{1,0:T(8,128)S(1)}, u32[]{:S(2)}, u32[]{:S(2)}) collective-permute-start(f32[16,128]{1,0:T(8,128)S(1)} %slice_select_fusion.1), channel_id=1, source_target_pairs={{0,1},{1,0},{2,3},{3,2},{4,5},{5,4},{6,7},{7,6},{8,9},{9,8},{10,11... | collective-permute-start | bytes 24584 | tf_op jit(solution)/shard_map/ppermute | solution.py:424
  31.9 3.7 %collective-permute-start.3 = (f32[32,128]{1,0:T(8,128)S(1)}, f32[32,128]{1,0:T(8,128)S(1)}, u32[]{:S(2)}, u32[]{:S(2)}) collective-permute-start(f32[32,128]{1,0:T(8,128)S(1)} %pad_maximum_fusion.1), channel_id=1, source_target_pairs={{0,8},{2,10},{4,12},{6,14},{8,0},{10,2},{12,4},{14,6},{16,24},{18,... | collective-permute-start | bytes 49160 | tf_op jit(solution)/shard_map/ppermute | solution.py:412
  35.6 4.7 %collective-permute-start.4 = (f32[32,128]{1,0:T(8,128)S(1)}, f32[32,128]{1,0:T(8,128)S(1)}, u32[]{:S(2)}, u32[]{:S(2)}) collective-permute-start(f32[32,128]{1,0:T(8,128)S(1)} %fusion), channel_id=1, source_target_pairs={{0,16},{2,18},{4,20},{6,22},{8,24},{10,26},{12,28},{14,30},{16,0},... | collective-permute-start | bytes 49160 | tf_op jit(solution)/shard_map/ppermute | solution.py:412
  40.3 3.7 %collective-permute-start.5 = (f32[32,128]{1,0:T(8,128)S(1)}, f32[32,128]{1,0:T(8,128)S(1)}, u32[]{:S(2)}, u32[]{:S(2)}) collective-permute-start(f32[32,128]{1,0:T(8,128)S(1)} %add.15), channel_id=1, source_target_pairs={{0,4},{2,6},{4,0},{6,2},{8,12},{10,14},{12,8},{14,10},{16,20},{18,... | collective-permute-start | bytes 49160 | tf_op jit(solution)/shard_map/ppermute | solution.py:432
  41.3 15.5 %collective-permute-start.7 = (f32[4,16,2048]{2,1,0:T(8,128)S(1)}, f32[4,16,2048]{2,1,0:T(8,128)S(1)}, u32[]{:S(2)}, u32[]{:S(2)}) collective-permute-start(f32[4,16,2048]{2,1,0:T(8,128)S(1)} %first_units.1.first_ref.own_first_ref), channel_id=1, source_target_pairs={{0,1},{1,0},{2,3},{3,2},{4,5},{5,4},{6,7},{7,6},{8,9},{9,8},{10,11... | collective-permute-start | bytes 1572872 | tf_op jit(solution)/shard_map/ppermute | solution.py:415
  43.0 15.5 %collective-permute-start.9 = (f32[2,16,2048]{2,1,0:T(8,128)S(1)}, f32[2,16,2048]{2,1,0:T(8,128)S(1)}, u32[]{:S(2)}, u32[]{:S(2)}) collective-permute-start(f32[2,16,2048]{2,1,0:T(8,128)S(1)} %get-tuple-element.18.own_last_ref), channel_id=1, source_target_pairs={{0,1},{1,0},{2,3},{3,2},{4,5},{5,4},{6,7},{7,6},{8,9},{9,8},{10,11... | collective-permute-start | bytes 786440 | tf_op jit(solution)/shard_map/ppermute | solution.py:426
  44.1 1.3 %collective-permute-start.6 = (f32[64,128]{1,0:T(8,128)S(1)}, f32[64,128]{1,0:T(8,128)S(1)}, u32[]{:S(2)}, u32[]{:S(2)}) collective-permute-start(f32[64,128]{1,0:T(8,128)S(1)} %pad_maximum_fusion.part_ref), channel_id=1, source_target_pairs={{0,2},{2,0},{4,6},{6,4},{8,10},{10,8},{12,14},{14,12},{16,18},{18,... | collective-permute-start | bytes 98312 | tf_op jit(solution)/shard_map/ppermute | solution.py:435
where the time goes:
time: 59.7 us; the launch traced here: 59.5 us
  waiting for transfers between devices  27.1 us (45%)
  Pallas kernels  17.1 us (29%)
  starting transfers between devices  15.1 us (25%)
    ppermute x1, waiting for transfers between devices, body(): oth = lax.ppermute(own, 'mem', swap)  20.6 us
    pallas_call x1, Pallas kernels, chain(): pl.pallas_call(chain_kernel, out_shape=[pltpu.VMEM((3 * half, 3 * k), jnp...  11.4 us
    ppermute x4, starting transfers between devices, across(): return lax.ppermute(x, 'tile', [(i, i ^ step) for i in range(n_tile)])  7.69 us
    ppermute x4, waiting for transfers between devices, across(): return lax.ppermute(x, 'tile', [(i, i ^ step) for i in range(n_tile)])  4.53 us
    ppermute x1, starting transfers between devices, body(): oth = lax.ppermute(own, 'mem', swap)  2.8 us
    pallas_call x1, Pallas kernels, gather_rows(): pl.pallas_call(gather_kernel, out_shape=(pltpu.VMEM((2 * half, batches *...  2.02 us
    ppermute x1, starting transfers between devices, body(): first = lax.ppermute(own_first, 'mem', swap)  1.74 us
    pallas_call x1, Pallas kernels, apply_matrix(): pl.pallas_call(apply_main, out_shape=(state, pltpu.VMEM((tail, half, cell...  1.67 us
  transfers between devices with their start and end apart: 10, of which 7 were waited for; matrix products, arithmetic and copies ran while one was open for 0% of the time, Pallas kernels for 22%

commit v1 on v0

--- a/solution.py
+++ b/solution.py
@@ -393,7 +393,7 @@
         in_specs=[VMEM, VMEM, VMEM, ANY],
         out_specs=ANY,
         input_output_aliases={3: 0},
-        scratch_shapes=[pltpu.VMEM((tail, half, cells), f32), pltpu.SemaphoreType.DMA((tail, 4))],
+        scratch_shapes=[pltpu.VMEM((tail, half, cells), f32), pltpu.SemaphoreType.DMA((tail, 2))],
         compiler_params=params,
         name="apply_last",
     )(vmem(theirs), vmem(part), vmem(last), hbm(out))
@@ -406,7 +406,7 @@
     ens = jnp.transpose(ensemble, (1, 0, 2))
     chans, half, cells = ens.shape
     units = ens.reshape(2 * chans, half // 2, cells)
-    head, tail = 4, 2
+    head, tail = 3, 2
 
     def across(x, step):
         return lax.ppermute(x, "tile", [(i, i ^ step) for i in range(n_tile)])
@@ -417,21 +417,14 @@
     own = own + across(own, 1)
     cut = own.shape[1] // 2
     own = jnp.where(lax.rem(tile[0], 2) == 0, own[:, :cut], own[:, cut:])
-    own = own + across(own, 2)
-    low = lax.rem(lax.div(tile[0], 2), 2) == 0
-    cut = own.shape[0] // 2
-    own = jnp.where(low, own[:cut], own[cut:])
     oth = lax.ppermute(own, "mem", swap)
     main = lax.ppermute(own_main, "mem", swap)
     last = lax.ppermute(own_last, "mem", swap)
     part = jnp.concatenate([own, oth], axis=0)
-    step = 4
+    step = 2
     while step < n_tile:
         part = part + across(part, step)
         step *= 2
-    other = lax.ppermute(part, "tile", [(i, i ^ 2) for i in range(n_tile)])
-    upper, lower = jnp.where(low, part, other), jnp.where(low, other, part)
-    part = jnp.concatenate([upper[:cut], lower[:cut], upper[cut:], lower[cut:]], axis=0)
     back = lax.ppermute(part, "tile", [(i, i ^ 1) for i in range(n_tile)])
     mat, mine, theirs = chain(part, back, obs_value, obs_var, owner_tile, tile_mask, batch_order, tile)
     out = apply_matrix(mat, mine, theirs, ens.shape, own_first, own_main, own_last, first, main, last)

time: 59.7 us -> 61.6 us (1.032)
  waiting for transfers between devices: 27.1 us -> 31.7 us
  starting transfers between devices: 15.1 us -> 12.4 us
    ppermute x1, waiting for transfers between devices: 20.6 us -> 23.9 us  [body(): oth = lax.ppermute(own, 'mem', swap)]
    ppermute x1, starting transfers between devices: 2.8 us -> 0.14 us  [body(): oth = lax.ppermute(own, 'mem', swap)]
    ppermute x4, waiting for transfers between devices: 4.53 us -> 6.67 us  [across(): return lax.ppermute(x, 'tile', [(i, i ^ step) for i in range(n_tile)])]
    ppermute x4, starting transfers between devices: 7.69 us -> 5.72 us  [across(): return lax.ppermute(x, 'tile', [(i, i ^ step) for i in range(n_tile)])]
    ppermute x1, starting transfers between devices: 1.52 us -> 3.06 us  [body(): main = lax.ppermute(own_main, 'mem', swap)]
    ppermute x1, starting transfers between devices: 0.28 us -> 1.52 us  [body(): last = lax.ppermute(own_last, 'mem', swap)]
    ppermute x1 -> x0, starting transfers between devices: 0.97 us -> none  [body(): other = lax.ppermute(part, 'tile', [(i, i ^ 2) for i in range(n_tile)])]
    ppermute x1 -> x0, waiting for transfers between devices: 0.74 us -> none  [body(): other = lax.ppermute(part, 'tile', [(i, i ^ 2) for i in range(n_tile)])]
  transfers between devices with their start and end apart: 10 -> 9, of which waited for: 7 -> 6; matrix products, arithmetic and copies ran while one was open for 0% -> 0% of each run, Pallas kernels for 22% -> 21%
where the time goes in v1:
time: 61.6 us; the launch traced here: 61.4 us
  waiting for transfers between devices  31.7 us (51%)
  Pallas kernels  17.1 us (28%)
  starting transfers between devices  12.4 us (20%)
    ppermute x1, waiting for transfers between devices, body(): oth = lax.ppermute(own, 'mem', swap)  23.9 us
    pallas_call x1, Pallas kernels, chain(): pl.pallas_call(chain_kernel, out_shape=[pltpu.VMEM((3 * half, 3 * k), jnp...  11.4 us
    ppermute x4, waiting for transfers between devices, across(): return lax.ppermute(x, 'tile', [(i, i ^ step) for i in range(n_tile)])  6.67 us
    ppermute x4, starting transfers between devices, across(): return lax.ppermute(x, 'tile', [(i, i ^ step) for i in range(n_tile)])  5.72 us
    ppermute x1, starting transfers between devices, body(): main = lax.ppermute(own_main, 'mem', swap)  3.06 us
    pallas_call x1, Pallas kernels, gather_rows(): pl.pallas_call(gather_kernel, out_shape=(pltpu.VMEM((2 * half, batches *...  2.06 us
    ppermute x1, starting transfers between devices, body(): first = lax.ppermute(own_first, 'mem', swap)  1.95 us
    pallas_call x1, Pallas kernels, apply_matrix(): pl.pallas_call(apply_main, out_shape=(state, pltpu.VMEM((tail, half, cell...  1.67 us
  transfers between devices with their start and end apart: 9, of which 6 were waited for; matrix products, arithmetic and copies ran while one was open for 0% of the time, Pallas kernels for 21%

profile of v1, /device:TPU:0, one launch (start us, length us, event | category | flops | bytes accessed | tf_op | source)
XLA Modules:
  0.0 61.4 jit_solution(17989887682913712707)
XLA Ops:
  0.0 1.0 %first_units.1.first_ref.own_first_ref = f32[3,16,2048]{2,1,0:T(8,128)S(1)} custom-call(f32[14,16,2048]{2,1,0:T(8,128)} %bitcast.5), custom_call_target="tpu_custom_call" | custom-call | tf_op jit(solution)/shard_map/first_units/pallas_call | solution.py:33
  1.0 0.0 copy-start
  1.0 0.0 copy-start.1
  1.0 0.0 copy-start.2
  1.0 0.0 copy-start.3
  1.1 0.0 copy-start.4
  1.1 2.1 %gather_rows.1 = (f32[32,256]{1,0:T(8,128)S(1)}, f32[9,16,2048]{2,1,0:T(8,128)S(1)}, f32[2,16,2048]{2,1,0:T(8,128)S(1)}) custom-call(s32[8,32]{1,0:T(8,128)} %site_hbm.1, s32[8]{0:T(128)} %owner_ref.1, s32[8]{0:T(128)} %order_ref.1, f32[14,16,2048]{2,1,0:T(8,128)} %bitcast.6, f32[3,16,2048]{2,1,0:T(8,128)S(1)} %first_units.1.first_ref.own_first_ref), custom_call_target="tpu_custom_call" | custom-call | tf_op jit(solution)/shard_map/gather_rows/pallas_call | solution.py:106
  3.1 3.1 %collective-permute-start.7 = (f32[9,16,2048]{2,1,0:T(8,128)S(1)}, f32[9,16,2048]{2,1,0:T(8,128)S(1)}, u32[]{:S(2)}, u32[]{:S(2)}) collective-permute-start(f32[9,16,2048]{2,1,0:T(8,128)S(1)} %get-tuple-element.17.own_main_ref), channel_id=1, source_target_pairs={{0,1},{1,0},{2,3},{3,2},{4,5},{5,4},{6,7},{7,6},{8,9},{9,8},{10,11... | collective-permute-start | bytes 3538952 | tf_op jit(solution)/shard_map/ppermute | solution.py:421
  6.2 0.0 collective-permute-start
  6.2 1.2 %collective-permute-done = f32[32,256]{1,0:T(8,128)S(1)} collective-permute-done((f32[32,256]{1,0:T(8,128)S(1)}, f32[32,256]{1,0:T(8,128)S(1)}, u32[]{:S(2)}, u32[]{:S(2)}) %collective-permute-start) | collective-permute-done | bytes 32800 | tf_op jit(solution)/shard_map/ppermute | solution.py:412
  7.4 0.1 collective-permute-start.1
  7.6 1.9 %collective-permute-start.6 = (f32[3,16,2048]{2,1,0:T(8,128)S(1)}, f32[3,16,2048]{2,1,0:T(8,128)S(1)}, u32[]{:S(2)}, u32[]{:S(2)}) collective-permute-start(f32[3,16,2048]{2,1,0:T(8,128)S(1)} %first_units.1.first_ref.own_first_ref), channel_id=1, source_target_pairs={{0,1},{1,0},{2,3},{3,2},{4,5},{5,4},{6,7},{7,6},{8,9},{9,8},{10,11... | collective-permute-start | bytes 1179656 | tf_op jit(solution)/shard_map/ppermute | solution.py:415
  9.5 23.9 %collective-permute-done.1 = f32[32,128]{1,0:T(8,128)S(1)} collective-permute-done((f32[32,128]{1,0:T(8,128)S(1)}, f32[32,128]{1,0:T(8,128)S(1)}, u32[]{:S(2)}, u32[]{:S(2)}) %collective-permute-start.1) | collective-permute-done | bytes 16416 | tf_op jit(solution)/shard_map/ppermute | solution.py:420
  33.4 1.3 %collective-permute-start.2 = (f32[64,128]{1,0:T(8,128)S(1)}, f32[64,128]{1,0:T(8,128)S(1)}, u32[]{:S(2)}, u32[]{:S(2)}) collective-permute-start(f32[64,128]{1,0:T(8,128)S(1)} %pad_maximum_fusion), channel_id=1, source_target_pairs={{0,4},{2,6},{4,0},{6,2},{8,12},{10,14},{12,8},{14,10},{16,20},{18,... | collective-permute-start | bytes 98312 | tf_op jit(solution)/shard_map/ppermute | solution.py:412
  34.7 1.5 %collective-permute-start.8 = (f32[2,16,2048]{2,1,0:T(8,128)S(1)}, f32[2,16,2048]{2,1,0:T(8,128)S(1)}, u32[]{:S(2)}, u32[]{:S(2)}) collective-permute-start(f32[2,16,2048]{2,1,0:T(8,128)S(1)} %get-tuple-element.18.own_last_ref), channel_id=1, source_target_pairs={{0,1},{1,0},{2,3},{3,2},{4,5},{5,4},{6,7},{7,6},{8,9},{9,8},{10,11... | collective-permute-start | bytes 786440 | tf_op jit(solution)/shard_map/ppermute | solution.py:422
  36.2 1.1 %collective-permute-done.2 = f32[64,128]{1,0:T(8,128)S(1)} collective-permute-done((f32[64,128]{1,0:T(8,128)S(1)}, f32[64,128]{1,0:T(8,128)S(1)}, u32[]{:S(2)}, u32[]{:S(2)}) %collective-permute-start.2) | collective-permute-done | bytes 32800 | tf_op jit(solution)/shard_map/ppermute | solution.py:412
  37.3 2.1 %collective-permute-start.3 = (f32[64,128]{1,0:T(8,128)S(1)}, f32[64,128]{1,0:T(8,128)S(1)}, u32[]{:S(2)}, u32[]{:S(2)}) collective-permute-start(f32[64,128]{1,0:T(8,128)S(1)} %fusion), channel_id=1, source_target_pairs={{0,8},{2,10},{4,12},{6,14},{8,0},{10,2},{12,4},{14,6},{16,24},{18,... | collective-permute-start | bytes 98312 | tf_op jit(solution)/shard_map/ppermute | solution.py:412
  39.4 1.9 %collective-permute-done.3 = f32[64,128]{1,0:T(8,128)S(1)} collective-permute-done((f32[64,128]{1,0:T(8,128)S(1)}, f32[64,128]{1,0:T(8,128)S(1)}, u32[]{:S(2)}, u32[]{:S(2)}) %collective-permute-start.3) | collective-permute-done | bytes 32800 | tf_op jit(solution)/shard_map/ppermute | solution.py:412
  41.3 2.3 %collective-permute-start.4 = (f32[64,128]{1,0:T(8,128)S(1)}, f32[64,128]{1,0:T(8,128)S(1)}, u32[]{:S(2)}, u32[]{:S(2)}) collective-permute-start(f32[64,128]{1,0:T(8,128)S(1)} %add.14), channel_id=1, source_target_pairs={{0,16},{2,18},{4,20},{6,22},{8,24},{10,26},{12,28},{14,30},{16,0},... | collective-permute-start | bytes 98312 | tf_op jit(solution)/shard_map/ppermute | solution.py:412
  43.6 2.5 %collective-permute-done.4 = f32[64,128]{1,0:T(8,128)S(1)} collective-permute-done((f32[64,128]{1,0:T(8,128)S(1)}, f32[64,128]{1,0:T(8,128)S(1)}, u32[]{:S(2)}, u32[]{:S(2)}) %collective-permute-start.4) | collective-permute-done | bytes 32800 | tf_op jit(solution)/shard_map/ppermute | solution.py:412
  46.1 0.0 collective-permute-start.5
  46.1 1.2 %collective-permute-done.5.back_ref = f32[64,128]{1,0:T(8,128)S(1)} collective-permute-done((f32[64,128]{1,0:T(8,128)S(1)}, f32[64,128]{1,0:T(8,128)S(1)}, u32[]{:S(2)}, u32[]{:S(2)}) %collective-permute-start.5) | collective-permute-done | bytes 32800 | tf_op jit(solution)/shard_map/ppermute | solution.py:428
  47.3 0.0 copy-done
  47.3 0.0 copy-done.1
  47.3 0.0 copy-done.2
  47.3 0.0 copy-done.3
  47.3 0.0 copy-done.4
  47.3 11.4 %chain.1 = (bf16[96,192]{1,0:T(8,128)(2,1)S(1)}, bf16[96,96]{1,0:T(8,128)(2,1)S(1)}, bf16[96,96]{1,0:T(8,128)(2,1)S(1)}) custom-call(s32[8]{0:T(128)S(1)} %copy-done.3, s32[8]{0:T(128)S(1)} %copy-done.4, s32[8,16]{1,0:T(8,128)S(1)} %copy-done, f32[8,32]{1,0:T(8,128)S(1)} %copy-done.1, s32[1]{0:T(128)} %bitcast.tile_ref, f32[64,128]{1,0:T(8,128)S(1)} %add.15.part_ref, ...), custom_call_target="tpu_custom_call" | custom-call | tf_op jit(solution)/shard_map/chain/pallas_call | solution.py:305
  58.8 0.0 collective-permute-done.6.first_ref
  58.8 0.0 collective-permute-done.7.main_ref
  58.8 1.7 %apply_main.1 = (f32[7,32,2048]{2,1,0:T(8,128)}, f32[1,32,2048]{2,1,0:T(8,128)S(1)}) custom-call(bf16[96,192]{1,0:T(8,128)(2,1)S(1)} %get-tuple-element.15.mat_ref, bf16[96,96]{1,0:T(8,128)(2,1)S(1)} %get-tuple-element.16.mine_ref, f32[3,16,2048]{2,1,0:T(8,128)S(1)} %first_units.1.first_ref.own_first_ref, f32[9,16,2048]{2,1,0:T(8,128)S(1)} %get-tuple-element.17.own_main_ref, ...), custom_call_target="tpu_custom_call" | custom-call | tf_op jit(solution)/shard_map/apply_main/pallas_call | solution.py:381
  60.5 0.0 collective-permute-done.8.last_ref
  60.5 0.9 %apply_last.1 = f32[7,32,2048]{2,1,0:T(8,128)} custom-call(bf16[96,96]{1,0:T(8,128)(2,1)S(1)} %get-tuple-element.14.theirs_ref, f32[1,32,2048]{2,1,0:T(8,128)S(1)} %get-tuple-element.19.part_ref, f32[2,16,2048]{2,1,0:T(8,128)S(1)} %collective-permute-done.8.last_ref, f32[7,32,2048]{2,1,0:T(8,128)} %get-tuple-element.20.prev_hbm), custom_call_target="tpu_custom_call", output_to_operand_aliasing={{}: (3, {})} | custom-call | tf_op jit(solution)/shard_map/apply_last/pallas_call | solution.py:390
  (6 shorter events, 0.0 us)
Async XLA Ops:
  1.0 46.3 %copy-start = (s32[8,16]{1,0:T(8,128)S(1)}, s32[8,16]{1,0:T(8,128)}, u32[]{:S(2)}) copy-start(s32[8,16]{1,0:T(8,128)} %mask_ref.1) | copy-start | bytes 1540
  1.0 46.3 %copy-start.1 = (f32[8,32]{1,0:T(8,128)S(1)}, f32[8,32]{1,0:T(8,128)}, u32[]{:S(2)}) copy-start(f32[8,32]{1,0:T(8,128)} %var_ref.1) | copy-start | bytes 3076
  1.0 46.3 %copy-start.2 = (f32[8,32]{1,0:T(8,128)S(1)}, f32[8,32]{1,0:T(8,128)}, u32[]{:S(2)}) copy-start(f32[8,32]{1,0:T(8,128)} %val_ref.1) | copy-start | bytes 3076
  1.0 46.3 %copy-start.3 = (s32[8]{0:T(128)S(1)}, s32[8]{0:T(128)}, u32[]{:S(2)}) copy-start(s32[8]{0:T(128)} %order_ref.1) | copy-start | bytes 100
  1.1 46.3 %copy-start.4 = (s32[8]{0:T(128)S(1)}, s32[8]{0:T(128)}, u32[]{:S(2)}) copy-start(s32[8]{0:T(128)} %owner_ref.1) | copy-start | bytes 100
  3.1 55.6 %collective-permute-start.7 = (f32[9,16,2048]{2,1,0:T(8,128)S(1)}, f32[9,16,2048]{2,1,0:T(8,128)S(1)}, u32[]{:S(2)}, u32[]{:S(2)}) collective-permute-start(f32[9,16,2048]{2,1,0:T(8,128)S(1)} %get-tuple-element.17.own_main_ref), channel_id=1, source_target_pairs={{0,1},{1,0},{2,3},{3,2},{4,5},{5,4},{6,7},{7,6},{8,9},{9,8},{10,11... | collective-permute-start | bytes 3538952 | tf_op jit(solution)/shard_map/ppermute | solution.py:421
  6.2 1.2 %collective-permute-start = (f32[32,256]{1,0:T(8,128)S(1)}, f32[32,256]{1,0:T(8,128)S(1)}, u32[]{:S(2)}, u32[]{:S(2)}) collective-permute-start(f32[32,256]{1,0:T(8,128)S(1)} %get-tuple-element.13), channel_id=1, source_target_pairs={{0,2},{2,0},{4,6},{6,4},{8,10},{10,8},{12,14},{14,12},{16,18},{18,... | collective-permute-start | bytes 98312 | tf_op jit(solution)/shard_map/ppermute | solution.py:412
  7.4 25.9 %collective-permute-start.1 = (f32[32,128]{1,0:T(8,128)S(1)}, f32[32,128]{1,0:T(8,128)S(1)}, u32[]{:S(2)}, u32[]{:S(2)}) collective-permute-start(f32[32,128]{1,0:T(8,128)S(1)} %slice_select_fusion), channel_id=1, source_target_pairs={{0,1},{1,0},{2,3},{3,2},{4,5},{5,4},{6,7},{7,6},{8,9},{9,8},{10,11... | collective-permute-start | bytes 49160 | tf_op jit(solution)/shard_map/ppermute | solution.py:420
  7.6 51.2 %collective-permute-start.6 = (f32[3,16,2048]{2,1,0:T(8,128)S(1)}, f32[3,16,2048]{2,1,0:T(8,128)S(1)}, u32[]{:S(2)}, u32[]{:S(2)}) collective-permute-start(f32[3,16,2048]{2,1,0:T(8,128)S(1)} %first_units.1.first_ref.own_first_ref), channel_id=1, source_target_pairs={{0,1},{1,0},{2,3},{3,2},{4,5},{5,4},{6,7},{7,6},{8,9},{9,8},{10,11... | collective-permute-start | bytes 1179656 | tf_op jit(solution)/shard_map/ppermute | solution.py:415
  33.4 3.9 %collective-permute-start.2 = (f32[64,128]{1,0:T(8,128)S(1)}, f32[64,128]{1,0:T(8,128)S(1)}, u32[]{:S(2)}, u32[]{:S(2)}) collective-permute-start(f32[64,128]{1,0:T(8,128)S(1)} %pad_maximum_fusion), channel_id=1, source_target_pairs={{0,4},{2,6},{4,0},{6,2},{8,12},{10,14},{12,8},{14,10},{16,20},{18,... | collective-permute-start | bytes 98312 | tf_op jit(solution)/shard_map/ppermute | solution.py:412
  34.7 25.8 %collective-permute-start.8 = (f32[2,16,2048]{2,1,0:T(8,128)S(1)}, f32[2,16,2048]{2,1,0:T(8,128)S(1)}, u32[]{:S(2)}, u32[]{:S(2)}) collective-permute-start(f32[2,16,2048]{2,1,0:T(8,128)S(1)} %get-tuple-element.18.own_last_ref), channel_id=1, source_target_pairs={{0,1},{1,0},{2,3},{3,2},{4,5},{5,4},{6,7},{7,6},{8,9},{9,8},{10,11... | collective-permute-start | bytes 786440 | tf_op jit(solution)/shard_map/ppermute | solution.py:422
  37.3 4.0 %collective-permute-start.3 = (f32[64,128]{1,0:T(8,128)S(1)}, f32[64,128]{1,0:T(8,128)S(1)}, u32[]{:S(2)}, u32[]{:S(2)}) collective-permute-start(f32[64,128]{1,0:T(8,128)S(1)} %fusion), channel_id=1, source_target_pairs={{0,8},{2,10},{4,12},{6,14},{8,0},{10,2},{12,4},{14,6},{16,24},{18,... | collective-permute-start | bytes 98312 | tf_op jit(solution)/shard_map/ppermute | solution.py:412
  41.3 4.8 %collective-permute-start.4 = (f32[64,128]{1,0:T(8,128)S(1)}, f32[64,128]{1,0:T(8,128)S(1)}, u32[]{:S(2)}, u32[]{:S(2)}) collective-permute-start(f32[64,128]{1,0:T(8,128)S(1)} %add.14), channel_id=1, source_target_pairs={{0,16},{2,18},{4,20},{6,22},{8,24},{10,26},{12,28},{14,30},{16,0},... | collective-permute-start | bytes 98312 | tf_op jit(solution)/shard_map/ppermute | solution.py:412
  46.1 1.2 %collective-permute-start.5 = (f32[64,128]{1,0:T(8,128)S(1)}, f32[64,128]{1,0:T(8,128)S(1)}, u32[]{:S(2)}, u32[]{:S(2)}) collective-permute-start(f32[64,128]{1,0:T(8,128)S(1)} %add.15.part_ref), channel_id=1, source_target_pairs={{0,2},{2,0},{4,6},{6,4},{8,10},{10,8},{12,14},{14,12},{16,18},{18,... | collective-permute-start | bytes 98312 | tf_op jit(solution)/shard_map/ppermute | solution.py:428
